TPU v7x, 32 devices: a whole 2x2x4 slice. The times are simulated.
32 devices in a mesh: vis: 4 (over y, core), row: 4 (over z), col: 2 (over x).
Axes of the slice: x: 2, y: 2, z: 4, core: 2. Of those that a mesh axis runs over, the one named last changes fastest.
Arguments:
- images: bfloat16 [128, 6400], P(('vis', 'row', 'col')), may hold values from -6 to 6
- counts: int32 [4], replicated, may hold values from 1 to 32, 64 in all
- block_order: int32 [4], replicated, may hold values from 0 to 3, each once
- projector_norm_gain: float32 [6400], replicated, may hold values from 0.1 to 1.9
- proj_first: bfloat16 [6400, 4096], P('vis', ('row', 'col')), may hold values from -0.078125 to 0.078125
- proj_bias: float32 [4096], P(('row', 'col')), may hold values from -3 to 3
- proj_second: bfloat16 [4096, 4096], P(('row', 'col'), 'vis'), may hold values from -0.09375 to 0.09375
- gate_weight: bfloat16 [4096, 16384], P('vis', ('row', 'col')), may hold values from -0.09375 to 0.09375
- up_weight: bfloat16 [4096, 16384], P('vis', ('row', 'col')), may hold values from -0.09375 to 0.09375
- down_weight: bfloat16 [16384, 4096], P(('row', 'col'), 'vis'), may hold values from -0.046875 to 0.046875
- cotangent: bfloat16 [64, 4096], P(('row', 'col'), 'vis'), may hold values from -6 to 6
Outputs:
- block_out: bfloat16 [64, 4096], P(('row', 'col'), 'vis')
- image_slot_gradients: float32 [128, 6400], P(('vis', 'row', 'col'))
- first_grad: float32 [6400, 4096], P('vis', ('row', 'col'))
- second_grad: float32 [4096, 4096], P(('row', 'col'), 'vis')
Inputs may be any that keep to these rules, and one draw needn't show every extreme that they name: Vision device v's live rows are its first counts[v] slots; the counts sum to 64, and some device's slots are all live. `block_order`: each vision device's index once: the order in which the devices' live rows follow one another among the language rows.
All inputs are finite; a program needn't handle non-finite values.
Results may differ from a plain program's by a relative error of at most 0.034.
Values may be sent and summed in bfloat16 or wider, within the bound.
A program may use at most 64 MiB of HBM per device.

v0:
```python
import jax
import jax.numpy as jnp
from jax import lax
from jax.sharding import PartitionSpec as P


def row_tables(counts, block_order, total_rows, per_device, group_size):
    vision = counts.shape[0]
    labels = jnp.arange(vision, dtype=jnp.int32)
    chosen = (block_order[:, None] == labels[None, :]).astype(jnp.int32)
    ordered = jnp.sum(chosen * counts[None, :], axis=1)
    block_ends = jnp.cumsum(ordered)
    block_starts = block_ends - ordered
    language = jnp.arange(total_rows, dtype=jnp.int32)
    block_of = jnp.sum((block_ends[None, :] <= language[:, None]).astype(jnp.int32), axis=1)
    picked = (block_of[:, None] == labels[None, :]).astype(jnp.int32)
    owner = jnp.sum(picked * block_order[None, :], axis=1)
    offset = language - jnp.sum(picked * block_starts[None, :], axis=1)
    stride = vision * per_device
    source = offset // per_device * stride + owner * per_device + offset % per_device
    slots = jnp.arange(stride * group_size, dtype=jnp.int32)
    within = slots % stride
    slot_owner = within // per_device
    slot_offset = slots // stride * per_device + within % per_device
    owner_start = jnp.sum(chosen * block_starts[:, None], axis=0)
    matched = (slot_owner[:, None] == labels[None, :]).astype(jnp.int32)
    start_of = jnp.sum(matched * owner_start[None, :], axis=1)
    count_of = jnp.sum(matched * counts[None, :], axis=1)
    live = slot_offset < count_of
    target = jnp.where(live, start_of + slot_offset, 0)
    return (source, target, live)


def gelu_parts(pre):
    normal_cdf = 0.5 * (1.0 + jax.scipy.special.erf(pre * 0.7071067811865476))
    density = jnp.exp(-0.5 * pre * pre) * 0.3989422804014327
    return (pre * normal_cdf, normal_cdf + pre * density)


def apply_layer_norm(images, projector_norm_gain):
    values = images.astype(jnp.float32)
    mean_removed = values - jnp.mean(values, axis=-1, keepdims=True)
    variance = jnp.mean(mean_removed * mean_removed, axis=-1, keepdims=True)
    inverse_scale = lax.rsqrt(variance + 1e-05)
    standardized_input = mean_removed * inverse_scale
    return (
        standardized_input,
        inverse_scale,
        (standardized_input * projector_norm_gain).astype(jnp.bfloat16),
    )


def norm_gradient_pass(gradient_tuple, standardized_input, inverse_scale, projector_norm_gain):
    gain_scaled = gradient_tuple * projector_norm_gain
    return inverse_scale * (
        gain_scaled
        - jnp.mean(gain_scaled, axis=-1, keepdims=True)
        - standardized_input * jnp.mean(gain_scaled * standardized_input, axis=-1, keepdims=True)
    )


def product(left, right):
    return jnp.dot(left, right, preferred_element_type=jnp.float32)


def feed_grads(hidden_grad, gate_sum, up_sum, gate_sigmoid):
    gate_grad = (
        hidden_grad * up_sum * gate_sigmoid * (1.0 + gate_sum * (1.0 - gate_sigmoid))
    ).astype(jnp.bfloat16)
    up_grad = (hidden_grad * gate_sum * gate_sigmoid).astype(jnp.bfloat16)
    return (gate_grad, up_grad)


def on_device(
    images,
    counts,
    block_order,
    projector_norm_gain,
    proj_first,
    proj_bias,
    proj_second,
    gate_weight,
    up_weight,
    down_weight,
    cotangent,
):
    group_size = lax.axis_size(("row", "col"))
    per_device = images.shape[0]
    local_rows = cotangent.shape[0]
    total_rows = local_rows * group_size
    position = lax.axis_index(("row", "col"))
    source, target, live = row_tables(counts, block_order, total_rows, per_device, group_size)
    standardized_input, inverse_scale, norm_output = apply_layer_norm(images, projector_norm_gain)
    columns = lax.all_to_all(norm_output, "vis", split_axis=1, concat_axis=0, tiled=True)
    gathered = lax.all_gather(columns, ("row", "col"), axis=0, tiled=True)
    first_part = jnp.take(product(gathered, proj_first), source, axis=0)
    pre = lax.psum(first_part.astype(jnp.bfloat16), "vis").astype(jnp.float32) + proj_bias
    activated, slope = gelu_parts(pre)
    hidden_proj = activated.astype(jnp.bfloat16)
    inputs = lax.psum(product(hidden_proj, proj_second).astype(jnp.bfloat16), ("row", "col"))
    gate_part = product(inputs, gate_weight)
    up_part = product(inputs, up_weight)
    gate_sum, up_sum = (
        lax.psum(gate_part.astype(jnp.bfloat16), "vis").astype(jnp.float32),
        lax.psum(up_part.astype(jnp.bfloat16), "vis").astype(jnp.float32),
    )
    gate_sigmoid = jax.nn.sigmoid(gate_sum)
    hidden = (gate_sum * gate_sigmoid * up_sum).astype(jnp.bfloat16)
    block_part = lax.psum_scatter(
        product(hidden, down_weight).astype(jnp.bfloat16),
        ("row", "col"),
        scatter_dimension=0,
        tiled=True,
    ).astype(jnp.float32)
    own_inputs = lax.dynamic_slice_in_dim(inputs, position * local_rows, local_rows, 0)
    block_out = (own_inputs.astype(jnp.float32) + block_part).astype(jnp.bfloat16)
    upstream = lax.all_gather(cotangent, ("row", "col"), axis=0, tiled=True)
    hidden_part = product(upstream, down_weight.T)
    hidden_grad = lax.psum(hidden_part.astype(jnp.bfloat16), "vis").astype(jnp.float32)
    gate_grad, up_grad = feed_grads(hidden_grad, gate_sum, up_sum, gate_sigmoid)
    input_part = product(gate_grad, gate_weight.T) + product(up_grad, up_weight.T)
    input_grad = (
        upstream.astype(jnp.float32)
        + lax.psum(input_part.astype(jnp.bfloat16), ("row", "col")).astype(jnp.float32)
    ).astype(jnp.bfloat16)
    second_grad = product(hidden_proj.T, input_grad)
    pre_part = product(input_grad, proj_second.T)
    pre_grad = lax.psum(pre_part.astype(jnp.bfloat16), "vis").astype(jnp.float32)
    act_grad = (pre_grad * slope).astype(jnp.bfloat16)
    slot_act = jnp.where(
        live[:, None], jnp.take(act_grad, target, axis=0), jnp.zeros((), jnp.bfloat16)
    )
    first_grad = product(gathered.T, slot_act)
    slot_part = lax.psum_scatter(
        product(slot_act, proj_first.T).astype(jnp.bfloat16),
        ("row", "col"),
        scatter_dimension=0,
        tiled=True,
    ).astype(jnp.float32)
    return_values = lax.all_to_all(slot_part, "vis", split_axis=0, concat_axis=1, tiled=True)
    image_slot_gradients = norm_gradient_pass(
        return_values, standardized_input, inverse_scale, projector_norm_gain
    )
    return (block_out, image_slot_gradients, first_grad, second_grad)


def solution(mesh):
    in_specs = (
        P(("vis", "row", "col"), None),
        P(),
        P(),
        P(),
        P("vis", ("row", "col")),
        P(("row", "col")),
        P(("row", "col"), "vis"),
        P("vis", ("row", "col")),
        P("vis", ("row", "col")),
        P(("row", "col"), "vis"),
        P(("row", "col"), "vis"),
    )
    out_specs = (
        P(("row", "col"), "vis"),
        P(("vis", "row", "col"), None),
        P("vis", ("row", "col")),
        P(("row", "col"), "vis"),
    )
    return jax.shard_map(
        on_device, mesh=mesh, in_specs=in_specs, out_specs=out_specs, check_vma=False
    )
```

profile of v0, /device:TPU:0, one launch (start us, length us, event | category | flops | bytes accessed | tf_op | source)
XLA Modules:
  0.0 442.7 jit_solution(14485268734717426963)
XLA Ops:
  7.2 1.1 convert_reduce_fusion
  8.3 1.0 fusion.33
  9.4 0.9 fusion.29
  11.1 4.3 all-to-all-start
  15.3 0.9 select_reduce_fusion.5
  17.3 2.1 all-to-all-done
  19.4 32.0 %all_gather.6 = bf16[128,1600]{1,0:T(8,128)(2,1)S(1)} all-gather(bf16[16,1600]{1,0:T(8,128)(2,1)S(1)} %all_to_all.33), channel_id=1, replica_groups=mesh['vis'=4,'row'=4,'col'=2] {'row','col'}, dimensions={0}, use_global_device_ids=true | all-gather | bytes 460800 | tf_op jit(solution)/shard_map/all_gather | solution.py:95
  53.3 30.7 %all_gather.7 = bf16[64,1024]{1,0:T(8,128)(2,1)S(1)} all-gather(bf16[8,1024]{1,0:T(8,128)(2,1)} %param.21), channel_id=1, replica_groups=mesh['vis'=4,'row'=4,'col'=2] {'row','col'}, dimensions={0}, use_global_device_ids=true | all-gather | bytes 147456 | tf_op jit(solution)/shard_map/all_gather | solution.py:117
  84.0 1.0 all-reduce.7.cloned.1.call-done
  85.0 1.8 convolution_convert_fusion.5
  86.9 4.3 convolution_convert_fusion.1
  91.3 68.2 %all-reduce.9.cloned.1.call-done = bf16[64,1024]{1,0:T(8,128)(2,1)} async-done(((bf16[64,1024]{1,0:T(8,128)(2,1)}), bf16[64,1024]{1,0:T(8,128)(2,1)}) %all-reduce.9.cloned.1.call-update) | async-done | bytes 131088 | tf_op jit(solution)/shard_map/psum | solution.py:100
  159.4 3.9 convolution_convert_fusion.2
  163.4 1.5 convolution_convert_fusion.3
  165.1 34.1 %all-reduce.15.cloned.1.call-done = (bf16[64,2048]{1,0:T(8,128)(2,1)}, bf16[64,2048]{1,0:T(8,128)(2,1)}, bf16[64,2048]{1,0:T(8,128)(2,1)}) async-done(((bf16[64,2048]{1,0:T(8,128)(2,1)}, bf16[64,2048]{1,0:T(8,128)(2,1)}, bf16[64,2048]{1,0:T(8,128)(2,1)}), (bf16[64,2048]{1,0:T(8,128)(2,1)}, bf16[64,2048]{1,0:T(8,128)(2,1)}, bf16[64,2048]{1,0:T(8,128)(2,1)})) %all-reduce.15.cloned.1.call-update) | async-done | bytes 786448 | tf_op jit(solution)/shard_map/psum | solution.py:105
  199.3 4.0 fusion.13
  203.3 2.1 fusion
  205.4 70.6 %all-reduce.11.cloned.1.call-done = bf16[64,1024]{1,0:T(8,128)(2,1)} async-done(((bf16[64,1024]{1,0:T(8,128)(2,1)}), bf16[64,1024]{1,0:T(8,128)(2,1)}) %all-reduce.11.cloned.1.call-update) | async-done | bytes 131088 | tf_op jit(solution)/shard_map/psum | solution.py:124
  276.0 2.0 convolution_convert_fusion.6
  278.0 31.3 %all-reduce.13.cloned.1.call-done = bf16[64,512]{1,0:T(8,128)(2,1)} async-done(((bf16[64,512]{1,0:T(8,128)(2,1)}), bf16[64,512]{1,0:T(8,128)(2,1)}) %all-reduce.13.cloned.1.call-update) | async-done | bytes 65552 | tf_op jit(solution)/shard_map/psum | solution.py:128
  309.4 0.9 fusion.23
  310.3 0.8 gather_fusion.1
  311.2 1.5 convolution_convert_fusion
  312.8 3.9 convolution_convert_fusion.4
  316.7 1.8 fusion.34
  318.5 2.4 fusion.48
  320.9 48.0 %reduce-scatter.5.cloned.1.call-done = bf16[16,1600]{1,0:T(8,128)(2,1)} async-done(((bf16[128,1600]{1,0:T(8,128)(2,1)}), bf16[16,1600]{1,0:T(8,128)(2,1)}) %reduce-scatter.5.cloned.1.call-update) | async-done | bytes 51216 | tf_op jit(solution)/shard_map/reduce_scatter | solution.py:134
  368.9 1.5 reshape.329
  370.4 3.3 all-to-all-start.1
  373.7 59.5 %reduce-scatter.3.cloned.1.call-done = bf16[8,1024]{1,0:T(8,128)(2,1)} async-done(((bf16[64,1024]{1,0:T(8,128)(2,1)}), bf16[8,1024]{1,0:T(8,128)(2,1)}) %reduce-scatter.3.cloned.1.call-update) | async-done | bytes 16400 | tf_op jit(solution)/shard_map/reduce_scatter | solution.py:109
  433.2 1.3 add_convert_fusion.3
  435.1 0.8 fusion.32
  (70 shorter events, 5.0 us)
Async XLA Ops:
  7.2 44.2 %copy-start = (bf16[1600,512]{1,0:T(8,128)(2,1)S(1)}, bf16[1600,512]{1,0:T(8,128)(2,1)}, u32[]{:S(2)}) copy-start(bf16[1600,512]{1,0:T(8,128)(2,1)} %param.15) | copy-start | bytes 4915204
  7.2 77.8 %copy-start.3 = (bf16[512,1024]{1,0:T(8,128)(2,1)S(1)}, bf16[512,1024]{1,0:T(8,128)(2,1)}, u32[]{:S(2)}) copy-start(bf16[512,1024]{1,0:T(8,128)(2,1)} %param.17) | copy-start | bytes 3145732
  7.2 77.8 %copy-start.9 = (f32[512]{0:T(512)S(1)}, f32[512]{0:T(512)}, u32[]{:S(2)}) copy-start(f32[512]{0:T(512)} %param.16) | copy-start | bytes 6148
  11.1 8.3 %all-to-all-start = ((bf16[4,4,1600]{2,0,1:T(4,128)(2,1)}), bf16[4,4,1600]{2,0,1:T(4,128)(2,1)S(1)}, u32[]{:S(2)}, u32[]{:S(2)}) async-start(bf16[4,4,1600]{2,0,1:T(4,128)(2,1)} %copy.18), calls=%async_computation | async-start | bytes 106496 | tf_op jit(solution)/shard_map/all_to_all | solution.py:94
  15.3 69.7 %all-reduce.7.cloned.1.call-start = ((), (), s32[]{:S(2)}) async-start(), calls=%async_computation.4 | async-start | bytes 131072 | tf_op jit(solution)/shard_map/psum | solution.py:97
  51.4 39.8 %copy-start.10 = (s32[4]{0:T(128)S(1)}, s32[4]{0:T(128)}, u32[]{:S(2)}) copy-start(s32[4]{0:T(128)} %param.13) | copy-start | bytes 52
  53.2 106.2 %all-reduce.9.cloned.1.call-start = ((), (), s32[]{:S(2)}) async-start(), calls=%async_computation.5 | async-start | bytes 262144 | tf_op jit(solution)/shard_map/psum | solution.py:100
  86.8 112.4 %all-reduce.15.cloned.1.call-start = ((), (), s32[]{:S(2)}) async-start(), calls=%async_computation.10 | async-start | bytes 1572864 | tf_op jit(solution)/shard_map/psum | solution.py:105
  91.3 73.8 %copy-start.11 = (s32[4]{0:T(128)S(1)}, s32[4]{0:T(128)}, u32[]{:S(2)}) copy-start(s32[4]{0:T(128)} %param.12) | copy-start | bytes 52
  159.4 4.0 copy-start.1
  159.4 4.0 copy-start.5
  165.0 111.0 %all-reduce.11.cloned.1.call-start = ((), (), s32[]{:S(2)}) async-start(), calls=%async_computation.7 | async-start | bytes 262144 | tf_op jit(solution)/shard_map/psum | solution.py:124
  199.2 4.0 copy-start.2
  199.3 4.0 copy-start.12
  199.3 4.0 copy-start.13
  203.2 106.1 %copy-start.6 = (bf16[64,512]{1,0:T(8,128)(2,1)S(1)}, bf16[64,512]{1,0:T(8,128)(2,1)}, u32[]{:S(2)}) copy-start(bf16[64,512]{1,0:T(8,128)(2,1)} %all-reduce.7.cloned.1.call-done) | copy-start | bytes 196612
  205.3 107.4 %copy-start.8 = (f32[6400]{0:T(1024)S(1)}, f32[6400]{0:T(1024)}, u32[]{:S(2)}) copy-start(f32[6400]{0:T(1024)} %param.14) | copy-start | bytes 76804
  205.3 104.0 %all-reduce.13.cloned.1.call-start = ((), (), s32[]{:S(2)}) async-start(), calls=%async_computation.8 | async-start | bytes 131072 | tf_op jit(solution)/shard_map/psum | solution.py:128
  278.0 90.9 %reduce-scatter.5.cloned.1.call-start = ((), (), s32[]{:S(2)}) async-start(), calls=%async_computation.9 | async-start | bytes 479232 | tf_op jit(solution)/shard_map/reduce_scatter | solution.py:134
  311.1 5.5 %copy-start.7 = (bf16[64,1024]{1,0:T(8,128)(2,1)S(1)}, bf16[64,1024]{1,0:T(8,128)(2,1)}, u32[]{:S(2)}) copy-start(bf16[64,1024]{1,0:T(8,128)(2,1)} %all-reduce.11.cloned.1.call-done) | copy-start | bytes 393220
  312.6 120.5 %reduce-scatter.3.cloned.1.call-start = ((), (), s32[]{:S(2)}) async-start(), calls=%async_computation.6 | async-start | bytes 147456 | tf_op jit(solution)/shard_map/reduce_scatter | solution.py:109
  316.7 118.0 %copy-start.4 = (bf16[4,6400]{1,0:T(4,128)(2,1)S(1)}, bf16[4,6400]{1,0:T(4,128)(2,1)}, u32[]{:S(2)}) copy-start(bf16[4,6400]{1,0:T(4,128)(2,1)} %param.11) | copy-start | bytes 153604
  370.4 64.1 %all-to-all-start.1 = ((f32[4,4,1600]{2,1,0:T(4,128)}), f32[4,4,1600]{2,1,0:T(4,128)S(1)}, u32[]{:S(2)}, u32[]{:S(2)}) async-start(f32[4,4,1600]{2,1,0:T(4,128)} %reshape.329), calls=%async_computation.3 | async-start | bytes 212992 | tf_op jit(solution)/shard_map/all_to_all | solution.py:140
Sparse Core Ops, SparseCore 0:
  53.3 31.6 all-reduce.6
  88.9 70.4 all-reduce.8
  165.1 34.1 all-reduce.14
  205.5 70.4 all-reduce.10
  278.7 30.6 all-reduce.12
  312.8 56.1 reduce-scatter.4
  372.2 60.9 reduce-scatter.2
where the time goes:
time: 443 us
  waiting for transfers between devices  315 us (71%)
  blocking collectives  62.7 us (14%)
  matrix products  29.5 us (7%)
  between operations  14.3 us (3%)
  other arithmetic  9.34 us (2%)
  starting transfers between devices  7.82 us (2%)
    psum x1, waiting for transfers between devices, on_device(): lax.psum(input_part.astype(jnp.bfloat16), ('row', 'col'))  70.6 us
    psum x1, waiting for transfers between devices, on_device(): lax.psum(product(hidden_proj, proj_second).astype(jnp.bfloat16), ('row',...  68.2 us
    reduce_scatter x1, waiting for transfers between devices, on_device(): lax.psum_scatter(product(hidden, down_weight).astype(jnp.bfloat16), ('row...  59.5 us
    reduce_scatter x1, waiting for transfers between devices, on_device(): lax.psum_scatter(product(slot_act, proj_first.T).astype(jnp.bfloat16), ('...  48 us
    psum x1, waiting for transfers between devices, on_device(): lax.psum(up_part.astype(jnp.bfloat16), 'vis').astype(jnp.float32)  34.1 us
    all_gather x1, blocking collectives, on_device(): gathered = lax.all_gather(columns, ('row', 'col'), axis=0, tiled=True)  32 us
    psum x1, waiting for transfers between devices, on_device(): lax.psum(pre_part.astype(jnp.bfloat16), 'vis').astype(jnp.float32)  31.3 us
    all_gather x1, blocking collectives, on_device(): upstream = lax.all_gather(cotangent, ('row', 'col'), axis=0, tiled=True)  30.7 us
  transfers between devices with their start and end apart: 9, of which 8 were waited for; matrix products, arithmetic and copies ran while one was open for 4% of the time, Pallas kernels for 0%

commit v1 on v0

--- a/solution.py
+++ b/solution.py
@@ -121,7 +121,9 @@
     input_part = product(gate_grad, gate_weight.T) + product(up_grad, up_weight.T)
     input_grad = (
         upstream.astype(jnp.float32)
-        + lax.psum(input_part.astype(jnp.bfloat16), ("row", "col")).astype(jnp.float32)
+        + jnp.sum(lax.all_gather(input_part.astype(jnp.bfloat16), ("row", "col")), axis=0).astype(
+            jnp.float32
+        )
     ).astype(jnp.bfloat16)
     second_grad = product(hidden_proj.T, input_grad)
     pre_part = product(input_grad, proj_second.T)

time: 443 us -> 421 us (0.950)
  waiting for transfers between devices: 315 us -> 292 us
    psum x1 -> x0, waiting for transfers between devices: 70.6 us -> none  [on_device(): lax.psum(input_part.astype(jnp.bfloat16), ('row', 'col'))]
    all_gather x0 -> x1, waiting for transfers between devices: none -> 40.1 us  [on_device(): lax.all_gather(input_part.astype(jnp.bfloat16), ('row', 'col'))]
    reduce_scatter x1, waiting for transfers between devices: 48 us -> 55.8 us  [on_device(): lax.psum_scatter(product(slot_act, proj_first.T).astype(jnp.bfloat16), ('...]
    psum x1, waiting for transfers between devices: 31.3 us -> 26.5 us  [on_device(): lax.psum(pre_part.astype(jnp.bfloat16), 'vis').astype(jnp.float32)]
  transfers between devices with their start and end apart: 9 -> 9, of which waited for: 8 -> 9; matrix products, arithmetic and copies ran while one was open for 4% -> 5% of each run, Pallas kernels for 0% -> 0%
where the time goes in v1:
time: 421 us
  waiting for transfers between devices  292 us (69%)
  blocking collectives  62.7 us (15%)
  matrix products  28.6 us (7%)
  between operations  14.3 us (3%)
  other arithmetic  10.8 us (3%)
  starting transfers between devices  7.83 us (2%)
    psum x1, waiting for transfers between devices, on_device(): lax.psum(product(hidden_proj, proj_second).astype(jnp.bfloat16), ('row',...  68.3 us
    reduce_scatter x1, waiting for transfers between devices, on_device(): lax.psum_scatter(product(hidden, down_weight).astype(jnp.bfloat16), ('row...  62.2 us
    reduce_scatter x1, waiting for transfers between devices, on_device(): lax.psum_scatter(product(slot_act, proj_first.T).astype(jnp.bfloat16), ('...  55.8 us
    all_gather x1, waiting for transfers between devices, on_device(): lax.all_gather(input_part.astype(jnp.bfloat16), ('row', 'col'))  40.1 us
    psum x1, waiting for transfers between devices, on_device(): lax.psum(up_part.astype(jnp.bfloat16), 'vis').astype(jnp.float32)  34.2 us
    all_gather x1, blocking collectives, on_device(): gathered = lax.all_gather(columns, ('row', 'col'), axis=0, tiled=True)  32 us
    all_gather x1, blocking collectives, on_device(): upstream = lax.all_gather(cotangent, ('row', 'col'), axis=0, tiled=True)  30.7 us
    dot_general x12, matrix products, product(): return jnp.dot(left, right, preferred_element_type=jnp.float32)  28.6 us
  transfers between devices with their start and end apart: 9, of which 9 were waited for; matrix products, arithmetic and copies ran while one was open for 5% of the time, Pallas kernels for 0%

profile of v1, /device:TPU:0, one launch (start us, length us, event | category | flops | bytes accessed | tf_op | source)
XLA Modules:
  0.0 420.7 jit_solution(10583916194462371126)
XLA Ops:
  7.2 1.1 convert_reduce_fusion
  8.3 1.0 fusion.33
  9.4 0.9 fusion.29
  11.1 4.3 %all-to-all-start = ((bf16[4,4,1600]{2,0,1:T(4,128)(2,1)}), bf16[4,4,1600]{2,0,1:T(4,128)(2,1)S(1)}, u32[]{:S(2)}, u32[]{:S(2)}) async-start(bf16[4,4,1600]{2,0,1:T(4,128)(2,1)} %copy.18), calls=%async_computation | async-start | bytes 106496 | tf_op jit(solution)/shard_map/all_to_all | solution.py:94
  15.3 0.9 select_reduce_fusion.5
  17.3 2.1 all-to-all-done
  19.4 32.0 %all_gather.12 = bf16[128,1600]{1,0:T(8,128)(2,1)S(1)} all-gather(bf16[16,1600]{1,0:T(8,128)(2,1)S(1)} %all_to_all.33), channel_id=1, replica_groups=mesh['vis'=4,'row'=4,'col'=2] {'row','col'}, dimensions={0}, use_global_device_ids=true | all-gather | bytes 460800 | tf_op jit(solution)/shard_map/all_gather | solution.py:95
  53.3 30.7 %all_gather.13 = bf16[64,1024]{1,0:T(8,128)(2,1)S(1)} all-gather(bf16[8,1024]{1,0:T(8,128)(2,1)} %param.21), channel_id=1, replica_groups=mesh['vis'=4,'row'=4,'col'=2] {'row','col'}, dimensions={0}, use_global_device_ids=true | all-gather | bytes 147456 | tf_op jit(solution)/shard_map/all_gather | solution.py:117
  84.0 1.0 all-reduce.6.cloned.1.call-done
  85.0 1.8 convolution_convert_fusion.5
  86.9 4.3 %convolution_convert_fusion.1 = bf16[64,2048]{1,0:T(8,128)(2,1)} fusion(bf16[64,1024]{1,0:T(8,128)(2,1)S(1)} %all_gather.13, bf16[2048,1024]{1,0:T(8,128)(2,1)} %param.20), kind=kOutput, calls=%fused_computation.3 | convolution fusion | flops 268566528 | bytes 4587520 | tf_op jit(solution)/shard_map/dot_general | solution.py:63
  91.2 68.3 %all-reduce.8.cloned.1.call-done = bf16[64,1024]{1,0:T(8,128)(2,1)} async-done(((bf16[64,1024]{1,0:T(8,128)(2,1)}), bf16[64,1024]{1,0:T(8,128)(2,1)}) %all-reduce.8.cloned.1.call-update) | async-done | bytes 131088 | tf_op jit(solution)/shard_map/psum | solution.py:100
  159.4 3.9 convolution_convert_fusion.2
  163.4 1.5 convolution_convert_fusion.3
  165.0 34.2 %all-reduce.12.cloned.1.call-done = (bf16[64,2048]{1,0:T(8,128)(2,1)}, bf16[64,2048]{1,0:T(8,128)(2,1)}, bf16[64,2048]{1,0:T(8,128)(2,1)}) async-done(((bf16[64,2048]{1,0:T(8,128)(2,1)}, bf16[64,2048]{1,0:T(8,128)(2,1)}, bf16[64,2048]{1,0:T(8,128)(2,1)}), (bf16[64,2048]{1,0:T(8,128)(2,1)}, bf16[64,2048]{1,0:T(8,128)(2,1)}, bf16[64,2048]{1,0:T(8,128)(2,1)})) %all-reduce.12.cloned.1.call-update) | async-done | bytes 786448 | tf_op jit(solution)/shard_map/psum | solution.py:105
  199.3 4.0 fusion.13
  203.3 2.1 fusion
  205.7 40.1 %all-gather.3.cloned.1.call-done = bf16[512,1024]{1,0:T(8,128)(2,1)} async-done(((bf16[64,1024]{1,0:T(8,128)(2,1)}), bf16[512,1024]{1,0:T(8,128)(2,1)}) %all-gather.3.cloned.1.call-update) | async-done | bytes 1048592 | tf_op jit(solution)/shard_map/all_gather | solution.py:124
  245.8 1.4 reduce_sum.127
  247.2 1.1 convolution_convert_fusion.6
  248.4 3.9 convolution_convert_fusion.4
  252.3 26.5 %all-reduce.10.cloned.1.call-done = bf16[64,512]{1,0:T(8,128)(2,1)} async-done(((bf16[64,512]{1,0:T(8,128)(2,1)}), bf16[64,512]{1,0:T(8,128)(2,1)}) %all-reduce.10.cloned.1.call-update) | async-done | bytes 65552 | tf_op jit(solution)/shard_map/psum | solution.py:130
  278.8 0.9 fusion.23
  280.6 1.5 convolution_convert_fusion
  282.2 62.2 %reduce-scatter.3.cloned.1.call-done = bf16[8,1024]{1,0:T(8,128)(2,1)} async-done(((bf16[64,1024]{1,0:T(8,128)(2,1)}), bf16[8,1024]{1,0:T(8,128)(2,1)}) %reduce-scatter.3.cloned.1.call-update) | async-done | bytes 16400 | tf_op jit(solution)/shard_map/reduce_scatter | solution.py:109
  344.4 1.3 add_convert_fusion.3
  345.7 1.8 fusion.34
  347.5 55.8 %reduce-scatter.5.cloned.1.call-done = bf16[16,1600]{1,0:T(8,128)(2,1)} async-done(((bf16[128,1600]{1,0:T(8,128)(2,1)}), bf16[16,1600]{1,0:T(8,128)(2,1)}) %reduce-scatter.5.cloned.1.call-update) | async-done | bytes 51216 | tf_op jit(solution)/shard_map/reduce_scatter | solution.py:136
  403.4 1.5 reshape.329
  404.8 3.3 all-to-all-start.1
  408.2 2.4 fusion.48
  410.5 1.9 all-to-all-done.1
  (69 shorter events, 6.6 us)
Async XLA Ops:
  7.2 44.2 %copy-start = (bf16[1600,512]{1,0:T(8,128)(2,1)S(1)}, bf16[1600,512]{1,0:T(8,128)(2,1)}, u32[]{:S(2)}) copy-start(bf16[1600,512]{1,0:T(8,128)(2,1)} %param.15) | copy-start | bytes 4915204
  7.2 77.8 %copy-start.3 = (bf16[512,1024]{1,0:T(8,128)(2,1)S(1)}, bf16[512,1024]{1,0:T(8,128)(2,1)}, u32[]{:S(2)}) copy-start(bf16[512,1024]{1,0:T(8,128)(2,1)} %param.17) | copy-start | bytes 3145732
  7.2 77.8 %copy-start.8 = (f32[512]{0:T(512)S(1)}, f32[512]{0:T(512)}, u32[]{:S(2)}) copy-start(f32[512]{0:T(512)} %param.16) | copy-start | bytes 6148
  11.1 8.3 %all-to-all-start = ((bf16[4,4,1600]{2,0,1:T(4,128)(2,1)}), bf16[4,4,1600]{2,0,1:T(4,128)(2,1)S(1)}, u32[]{:S(2)}, u32[]{:S(2)}) async-start(bf16[4,4,1600]{2,0,1:T(4,128)(2,1)} %copy.18), calls=%async_computation | async-start | bytes 106496 | tf_op jit(solution)/shard_map/all_to_all | solution.py:94
  15.3 69.7 %all-reduce.6.cloned.1.call-start = ((), (), s32[]{:S(2)}) async-start(), calls=%async_computation.4 | async-start | bytes 131072 | tf_op jit(solution)/shard_map/psum | solution.py:97
  53.2 106.2 %all-reduce.8.cloned.1.call-start = ((), (), s32[]{:S(2)}) async-start(), calls=%async_computation.5 | async-start | bytes 262144 | tf_op jit(solution)/shard_map/psum | solution.py:100
  86.8 112.4 %all-reduce.12.cloned.1.call-start = ((), (), s32[]{:S(2)}) async-start(), calls=%async_computation.10 | async-start | bytes 1572864 | tf_op jit(solution)/shard_map/psum | solution.py:105
  159.4 4.0 copy-start.1
  159.4 4.0 copy-start.5
  165.0 80.8 %all-gather.3.cloned.1.call-start = ((), (), s32[]{:S(2)}) async-start(), calls=%async_computation.9 | async-start | bytes 1179648 | tf_op jit(solution)/shard_map/all_gather | solution.py:124
  199.3 4.0 copy-start.2
  199.3 4.0 copy-start.11
  199.3 4.0 copy-start.12
  203.3 2.2 copy-start.9
  203.3 2.3 copy-start.10
  205.4 73.4 %all-reduce.10.cloned.1.call-start = ((), (), s32[]{:S(2)}) async-start(), calls=%async_computation.7 | async-start | bytes 131072 | tf_op jit(solution)/shard_map/psum | solution.py:130
  248.3 30.5 %copy-start.6 = (bf16[64,512]{1,0:T(8,128)(2,1)S(1)}, bf16[64,512]{1,0:T(8,128)(2,1)}, u32[]{:S(2)}) copy-start(bf16[64,512]{1,0:T(8,128)(2,1)} %all-reduce.6.cloned.1.call-done) | copy-start | bytes 196612
  248.3 33.8 %copy-start.7 = (f32[6400]{0:T(1024)S(1)}, f32[6400]{0:T(1024)}, u32[]{:S(2)}) copy-start(f32[6400]{0:T(1024)} %param.14) | copy-start | bytes 76804
  248.3 96.1 %reduce-scatter.3.cloned.1.call-start = ((), (), s32[]{:S(2)}) async-start(), calls=%async_computation.6 | async-start | bytes 147456 | tf_op jit(solution)/shard_map/reduce_scatter | solution.py:109
  252.3 151.1 %reduce-scatter.5.cloned.1.call-start = ((), (), s32[]{:S(2)}) async-start(), calls=%async_computation.8 | async-start | bytes 479232 | tf_op jit(solution)/shard_map/reduce_scatter | solution.py:136
  282.0 130.6 %copy-start.4 = (bf16[4,6400]{1,0:T(4,128)(2,1)S(1)}, bf16[4,6400]{1,0:T(4,128)(2,1)}, u32[]{:S(2)}) copy-start(bf16[4,6400]{1,0:T(4,128)(2,1)} %param.11) | copy-start | bytes 153604
  404.8 7.6 %all-to-all-start.1 = ((f32[4,4,1600]{2,1,0:T(4,128)}), f32[4,4,1600]{2,1,0:T(4,128)S(1)}, u32[]{:S(2)}, u32[]{:S(2)}) async-start(f32[4,4,1600]{2,1,0:T(4,128)} %reshape.329), calls=%async_computation.3 | async-start | bytes 212992 | tf_op jit(solution)/shard_map/all_to_all | solution.py:142
Sparse Core Ops, SparseCore 0:
  53.3 31.6 all-reduce.5
  88.9 70.4 all-reduce.7
  165.1 34.1 all-reduce.11
  205.5 40.2 all-gather.2
  248.5 30.2 all-reduce.9
  282.6 61.8 reduce-scatter.2
  348.2 55.1 reduce-scatter.4
